TPU v7x, 32 devices: a whole 2x2x4 slice. The times are simulated.
32 devices in a mesh: row: 8 (over z, core), col: 4 (over y, x).
Axes of the slice: x: 2, y: 2, z: 4, core: 2. Of those that a mesh axis runs over, the one named last changes fastest.
Arguments:
- alignment: bfloat16 [256, 16384], P('row', 'col'), may hold values from -6 to 6
- pair_state: float32 [256, 256, 128], P('row', 'col'), may hold values from -6 to 6
- alignment_factor_weight: bfloat16 [64, 64], replicated, may hold values from -0.75 to 0.75
- outer_proj: bfloat16 [1024, 128], replicated, may hold values from -3 to 3
- outgoing_proj: bfloat16 [128, 640], replicated, may hold values from -0.5 to 0.5
- outgoing_final: bfloat16 [128, 128], replicated, may hold values from -0.5 to 0.5
- incoming_proj: bfloat16 [128, 640], replicated, may hold values from -0.5 to 0.5
- incoming_final: bfloat16 [128, 128], replicated, may hold values from -0.5 to 0.5
Outputs:
- pair_result: float32 [256, 256, 128], P('row', 'col')
All inputs are finite; a program needn't handle non-finite values.
Results may differ from a plain program's by a relative error of at most 0.0065.
Values may be sent and summed in bfloat16 or wider, within the bound.
No kernel may reach another device: no remote copies, remote signals or barrier semaphores. Data moves between devices by JAX's collectives and lax.ppermute only.
A program may use at most 128 MiB of HBM per device.

v0:
```python
import jax
import jax.numpy as jnp
from jax import lax
from jax.sharding import PartitionSpec as P

epsilon = 1e-05


def normalize_layer(values):
    average = jnp.mean(values, axis=-1, keepdims=True)
    centred = values - average
    spread = jnp.mean(centred * centred, axis=-1, keepdims=True)
    return centred * lax.rsqrt(spread + epsilon)


def project_pair(pair_now, weights, hidden_dim):
    rows_here, cols_here, channels = pair_now.shape
    normed_in = normalize_layer(pair_now).astype(jnp.bfloat16).reshape(-1, channels)
    projected = jnp.dot(normed_in, weights, preferred_element_type=jnp.float32).reshape(
        rows_here, cols_here, -1
    )
    left_factor = (
        jax.nn.sigmoid(projected[..., :hidden_dim]) * projected[..., hidden_dim : 2 * hidden_dim]
    ).astype(jnp.bfloat16)
    right_factor = (
        jax.nn.sigmoid(projected[..., 2 * hidden_dim : 3 * hidden_dim])
        * projected[..., 3 * hidden_dim : 4 * hidden_dim]
    ).astype(jnp.bfloat16)
    gate_vals = jax.nn.sigmoid(projected[..., 4 * hidden_dim :])
    return (left_factor, right_factor, gate_vals)


def finish_pair(pair_now, mixed_sum, gate_vals, final_weights):
    rows_here, cols_here, channels = pair_now.shape
    normed_mix = normalize_layer(mixed_sum).astype(jnp.bfloat16).reshape(-1, mixed_sum.shape[-1])
    update = jnp.dot(normed_mix, final_weights, preferred_element_type=jnp.float32).reshape(
        rows_here, cols_here, channels
    )
    return pair_now + gate_vals * update


def channel_major(tile):
    return jnp.transpose(tile, (2, 0, 1))


def assemble_full(received, row_count, col_count, row_tokens, col_tokens):
    share = received.shape[0]
    shaped = received.reshape(share, row_count, col_count, row_tokens, col_tokens)
    return shaped.transpose(0, 1, 3, 2, 4).reshape(
        share, row_count * row_tokens, col_count * col_tokens
    )


def split_tiles(mixed_full, row_count, col_count, row_tokens, col_tokens):
    share = mixed_full.shape[0]
    shaped = mixed_full.reshape(share, row_count, row_tokens, col_count, col_tokens)
    return shaped.transpose(1, 3, 2, 4, 0).reshape(
        row_count * col_count * row_tokens, col_tokens, share
    )


def local(
    alignment,
    pair_state,
    alignment_factor_weight,
    outer_proj,
    outgoing_proj,
    outgoing_final,
    incoming_proj,
    incoming_final,
):
    seq_local = alignment.shape[0]
    row_tokens, col_tokens, channels = pair_state.shape
    feature_width = alignment_factor_weight.shape[0]
    hidden_outer = alignment_factor_weight.shape[1] // 2
    hidden_dim = outgoing_final.shape[0]
    row_count = lax.axis_size("row")
    col_count = lax.axis_size("col")
    seq_total = seq_local * row_count
    feature_values = alignment.astype(jnp.float32).reshape(seq_local, col_tokens, feature_width)
    normalized_alignment = (
        normalize_layer(feature_values).astype(jnp.bfloat16).reshape(-1, feature_width)
    )
    factor_pairs = jnp.dot(
        normalized_alignment, alignment_factor_weight, preferred_element_type=jnp.float32
    ).astype(jnp.bfloat16)
    factor_pairs = factor_pairs.reshape(seq_local, col_tokens, 2 * hidden_outer)
    row_source = factor_pairs[:, :, :hidden_outer].reshape(seq_local, col_tokens * hidden_outer)
    col_source = factor_pairs[:, :, hidden_outer:].reshape(seq_local, col_tokens * hidden_outer)
    all_tokens = lax.all_gather(row_source, "col", axis=1, tiled=True)
    row_factor = lax.all_to_all(all_tokens, "row", split_axis=1, concat_axis=0, tiled=True)
    outer_sum = lax.dot_general(
        row_factor,
        lax.all_gather(col_source, "row", axis=0, tiled=True),
        (((0,), (0,)), ((), ())),
        preferred_element_type=jnp.float32,
    )
    outer_mean = (
        (outer_sum / seq_total)
        .astype(jnp.bfloat16)
        .reshape(row_tokens, hidden_outer, col_tokens, hidden_outer)
    )
    outer_mean = outer_mean.transpose(0, 2, 1, 3).reshape(
        row_tokens * col_tokens, hidden_outer * hidden_outer
    )
    opm_term = jnp.dot(outer_mean, outer_proj, preferred_element_type=jnp.float32).reshape(
        row_tokens, col_tokens, channels
    )
    pair_opm = pair_state + opm_term
    left_factor, right_factor, gate_vals = project_pair(pair_opm, outgoing_proj, hidden_dim)
    col_panel = lax.all_gather(right_factor, "row", axis=0, tiled=True)
    right_factor_rows = lax.all_to_all(col_panel, "col", split_axis=0, concat_axis=1, tiled=True)
    mixed_out = jnp.einsum(
        "ikc,jkc->ijc",
        lax.all_gather(left_factor, "col", axis=1, tiled=True),
        right_factor_rows,
        preferred_element_type=jnp.float32,
    )
    pair_mid = finish_pair(pair_opm, mixed_out, gate_vals, outgoing_final)
    left_factor, right_factor, gate_vals = project_pair(pair_mid, incoming_proj, hidden_dim)
    left_share, right_share = (
        lax.all_to_all(
            channel_major(left_factor), ("row", "col"), split_axis=0, concat_axis=1, tiled=True
        ),
        lax.all_to_all(
            channel_major(right_factor), ("row", "col"), split_axis=0, concat_axis=1, tiled=True
        ),
    )
    left_full = assemble_full(left_share, row_count, col_count, row_tokens, col_tokens)
    right_full = assemble_full(right_share, row_count, col_count, row_tokens, col_tokens)
    mixed_full = jnp.einsum(
        "cki,ckj->cij", left_full, right_full, preferred_element_type=jnp.float32
    )
    mixed_in = lax.all_to_all(
        split_tiles(mixed_full, row_count, col_count, row_tokens, col_tokens).astype(jnp.bfloat16),
        ("row", "col"),
        split_axis=0,
        concat_axis=2,
        tiled=True,
    ).astype(jnp.float32)
    return finish_pair(pair_mid, mixed_in, gate_vals, incoming_final)


def solution(mesh):
    return jax.shard_map(
        local,
        mesh=mesh,
        in_specs=(P("row", "col"), P("row", "col", None), P(), P(), P(), P(), P(), P()),
        out_specs=P("row", "col", None),
        check_vma=False,
    )
```

profile of v0, /device:TPU:0, one launch (start us, length us, event | category | flops | bytes accessed | tf_op | source)
XLA Modules:
  0.0 318.9 jit_solution(2748084804369626462)
XLA Ops:
  6.5 1.4 reshape.155
  8.3 0.6 multiply_reduce_fusion.4
  9.6 0.8 convolution_convert_fusion
  10.9 1.2 reshape.158
  12.2 0.5 reshape.157
  12.7 11.5 %all_gather.12 = bf16[32,8192]{1,0:T(8,128)(2,1)S(1)} all-gather(bf16[32,2048]{1,0:T(8,128)(2,1)S(1)} %reshape.157), channel_id=1, replica_groups=mesh['row'=8,'col'=4] {'col'}, dimensions={1}, use_global_device_ids=true | all-gather | bytes 655360 | tf_op jit(solution)/shard_map/all_gather | solution.py:90
  24.3 22.2 %all_to_all.76 = bf16[32,8,1024]{2,0,1:T(8,128)(2,1)S(1)} all-to-all(bf16[32,8,1024]{2,0,1:T(8,128)(2,1)S(1)} %bitcast.104), channel_id=1, replica_groups=mesh['row'=8,'col'=4] {'row'}, dimensions={1} | all-to-all | bytes 1048576 | tf_op jit(solution)/shard_map/all_to_all | solution.py:91
  46.5 4.5 %multiply_convert_fusion = bf16[1024,2048]{1,0:T(8,128)(2,1)} fusion(bf16[256,1024]{1,0:T(8,128)(2,1)S(1)} %bitcast.105, bf16[256,2048]{1,0:T(8,128)(2,1)} %all-gather.4.cloned.1.call-done), kind=kOutput, calls=%fused_computation | convolution fusion | flops 1077936128 | bytes 5767168 | tf_op jit(solution)/shard_map/dot_general | solution.py:92
  50.9 19.5 %reshape.159 = bf16[32,32,64,32]{3,2,1,0:T(8,128)(2,1)} reshape(bf16[1024,2048]{1,0:T(8,128)(2,1)} %multiply_convert_fusion) | data formatting | bytes 8388608 | tf_op jit(solution)/shard_map/reshape | solution.py:101
  70.4 16.0 %copy.53 = bf16[32,64,32,32]{1,3,2,0:T(8,128)(2,1)} copy(bf16[32,64,32,32]{3,1,2,0:T(8,128)(2,1)} %bitcast.91) | data formatting | bytes 8388608 | tf_op jit(solution)/shard_map/transpose | solution.py:103
  86.5 6.0 %fusion.46 = (f32[32,64]{1,0:T(8,128)S(1)}, f32[32,64,128]{2,1,0:T(8,128)S(1)}) fusion(f32[32,64,128]{2,1,0:T(8,128)S(1)} %copy-done.4, bf16[32,64,1024]{1,2,0:T(8,128)(2,1)} %bitcast.90, bf16[1024,128]{1,0:T(8,128)(2,1)S(1)} %copy-done), kind=kOutput, calls=%fused_computation.88 | convolution fusion | flops 537393152 | bytes 6561792 | tf_op jit(solution)/shard_map/dot_general | solution.py:106
  92.5 0.6 multiply_reduce_fusion.3
  93.1 1.0 fusion.29
  94.2 1.9 fusion.16
  96.1 0.8 copy-done.3
  96.9 0.7 all-gather.8.cloned.1.call-update
  97.6 45.5 %all-gather.6.cloned.1.call-done = bf16[256,64,128]{2,1,0:T(8,128)(2,1)} async-done(((bf16[32,64,128]{2,1,0:T(8,128)(2,1)}), bf16[256,64,128]{2,1,0:T(8,128)(2,1)}) %all-gather.6.cloned.1.call-update) | async-done | bytes 4194320 | tf_op jit(solution)/shard_map/all_gather | solution.py:111
  143.1 5.0 %all-to-all-start.1 = ((bf16[256,64,128]{2,1,0:T(8,128)(2,1)}), bf16[256,64,128]{2,1,0:T(8,128)(2,1)}, u32[]{:S(2)}, u32[]{:S(2)}) async-start(bf16[256,64,128]{2,1,0:T(8,128)(2,1)} %all-gather.6.cloned.1.call-done), calls=%async_computation.1 | async-start | bytes 8388608 | tf_op jit(solution)/shard_map/all_to_all | solution.py:112
  148.1 64.6 %all-gather.8.cloned.1.call-done = bf16[32,256,128]{2,1,0:T(8,128)(2,1)} async-done(((bf16[32,64,128]{2,1,0:T(8,128)(2,1)}), bf16[32,256,128]{2,1,0:T(8,128)(2,1)}) %all-gather.8.cloned.1.call-update) | async-done | bytes 2097168 | tf_op jit(solution)/shard_map/all_gather | solution.py:115
  212.8 3.4 %copy.57 = bf16[32,256,128]{1,0,2:T(8,128)(2,1)S(1)} copy(bf16[32,256,128]{2,1,0:T(8,128)(2,1)} %all-gather.8.cloned.1.call-done) | data formatting | bytes 4194304 | tf_op jit(solution)/shard_map/all_gather | solution.py:115
  216.2 5.6 %copy.55 = bf16[64,4,64,128]{3,2,1,0:T(8,128)(2,1)} copy(bf16[64,4,64,128]{3,2,0,1:T(8,128)(2,1)} %bitcast.7) | data formatting | bytes 8388608 | tf_op jit(solution)/shard_map/all_to_all | solution.py:112
  221.8 6.8 %copy.56 = bf16[64,256,128]{1,0,2:T(8,128)(2,1)} copy(bf16[64,256,128]{2,1,0:T(8,128)(2,1)} %bitcast.92) | data formatting | bytes 8388608 | tf_op jit(solution)/shard_map/all_to_all | solution.py:112
  228.6 3.4 %bitcast_reduce_fusion = (f32[32,64]{1,0:T(8,128)S(1)}, f32[128,64,32]{1,2,0:T(8,128)S(1)}) fusion(bf16[64,256,128]{1,0,2:T(8,128)(2,1)} %copy.56, bf16[32,256,128]{1,0,2:T(8,128)(2,1)S(1)} %copy.57), kind=kOutput, calls=%fused_computation.7 | convolution fusion | flops 134477824 | bytes 7348224 | tf_op jit(solution)/shard_map/ikc,jkc->ijc/dot_general | solution.py:113
  233.1 2.0 fusion.47
  235.2 0.6 multiply_reduce_fusion.2
  235.9 1.0 fusion.30
  236.9 0.6 fusion.38
  237.5 1.7 copy-done.2
  239.2 1.6 copy.61
  240.8 1.6 reshape.174
  242.4 2.9 all-to-all-start.3
  245.3 1.6 copy.59
  247.0 1.5 reshape.172
  248.5 13.1 %all-to-all-done.3 = bf16[32,2,4096]{2,1,0:T(2,128)(2,1)S(1)} async-done(((bf16[32,2,4096]{2,1,0:T(2,128)(2,1)}), bf16[32,2,4096]{2,1,0:T(2,128)(2,1)S(1)}, u32[]{:S(2)}, u32[]{:S(2)}) %all-to-all-start.3) | async-done | bytes 524320 | tf_op jit(solution)/shard_map/all_to_all | solution.py:125
  261.6 3.6 %all-to-all-start.2 = ((bf16[32,2,4096]{2,1,0:T(2,128)(2,1)}), bf16[32,2,4096]{2,1,0:T(2,128)(2,1)}, u32[]{:S(2)}, u32[]{:S(2)}) async-start(bf16[32,2,4096]{2,1,0:T(2,128)(2,1)} %reshape.172), calls=%async_computation.2 | async-start | bytes 1048576 | tf_op jit(solution)/shard_map/all_to_all | solution.py:122
  265.2 0.7 reshape.175
  265.8 0.8 copy.85
  266.7 1.5 reshape.163
  268.1 13.1 %all-to-all-done.2 = bf16[32,2,4096]{2,1,0:T(2,128)(2,1)} async-done(((bf16[32,2,4096]{2,1,0:T(2,128)(2,1)}), bf16[32,2,4096]{2,1,0:T(2,128)(2,1)}, u32[]{:S(2)}, u32[]{:S(2)}) %all-to-all-start.2) | async-done | bytes 524320 | tf_op jit(solution)/shard_map/all_to_all | solution.py:122
  281.2 2.3 reshape.173
  283.5 0.8 copy.86
  284.3 0.7 reshape.161
  285.0 1.4 convolution_convert_fusion.1
  287.0 0.8 copy.88
  287.9 0.7 reshape.176
  288.6 18.3 %all_to_all.77 = bf16[32,2,4096]{2,1,0:T(2,128)(2,1)S(1)} all-to-all(bf16[32,2,4096]{2,1,0:T(2,128)(2,1)S(1)} %reshape.176), channel_id=1, replica_groups=mesh['row'=8,'col'=4] {'row','col'}, dimensions={0} | all-to-all | bytes 1048576 | tf_op jit(solution)/shard_map/all_to_all | solution.py:134
  306.9 0.7 reshape.177
  309.5 2.8 fusion.2
  (53 shorter events, 5.3 us)
Async XLA Ops:
  6.5 79.9 %copy-start = (bf16[1024,128]{1,0:T(8,128)(2,1)S(1)}, bf16[1024,128]{1,0:T(8,128)(2,1)}, u32[]{:S(2)}) copy-start(bf16[1024,128]{1,0:T(8,128)(2,1)} %param.11) | copy-start | bytes 786436
  6.5 2.5 copy-start.5
  6.5 39.9 %all-gather.4.cloned.1.call-start = ((), (), s32[]{:S(2)}) async-start(), calls=%async_computation.5 | async-start | bytes 1179648 | tf_op jit(solution)/shard_map/all_gather | solution.py:94
  8.0 1.6 copy-start.8
  12.1 131.0 %all-gather.6.cloned.1.call-start = ((), (), s32[]{:S(2)}) async-start(), calls=%async_computation.6 | async-start | bytes 4718592 | tf_op jit(solution)/shard_map/all_gather | solution.py:111
  70.4 16.0 %copy-start.4 = (f32[32,64,128]{2,1,0:T(8,128)S(1)}, f32[32,64,128]{2,1,0:T(8,128)}, u32[]{:S(2)}) copy-start(f32[32,64,128]{2,1,0:T(8,128)} %param.9) | copy-start | bytes 3145732
  86.5 6.7 %copy-start.6 = (bf16[128,640]{1,0:T(8,128)(2,1)S(1)}, bf16[128,640]{1,0:T(8,128)(2,1)}, u32[]{:S(2)}) copy-start(bf16[128,640]{1,0:T(8,128)(2,1)} %param.12) | copy-start | bytes 491524
  94.2 2.6 copy-start.3
  96.8 115.9 %all-gather.8.cloned.1.call-start = ((), (), s32[]{:S(2)}) async-start(), calls=%async_computation.7 | async-start | bytes 2621440 | tf_op jit(solution)/shard_map/all_gather | solution.py:115
  143.1 73.1 %all-to-all-start.1 = ((bf16[256,64,128]{2,1,0:T(8,128)(2,1)}), bf16[256,64,128]{2,1,0:T(8,128)(2,1)}, u32[]{:S(2)}, u32[]{:S(2)}) async-start(bf16[256,64,128]{2,1,0:T(8,128)(2,1)} %all-gather.6.cloned.1.call-done), calls=%async_computation.1 | async-start | bytes 8388608 | tf_op jit(solution)/shard_map/all_to_all | solution.py:112
  232.4 0.8 copy-start.9
  233.1 2.7 copy-start.7
  236.9 2.3 copy-start.2
  242.4 19.2 %all-to-all-start.3 = ((bf16[32,2,4096]{2,1,0:T(2,128)(2,1)}), bf16[32,2,4096]{2,1,0:T(2,128)(2,1)S(1)}, u32[]{:S(2)}, u32[]{:S(2)}) async-start(bf16[32,2,4096]{2,1,0:T(2,128)(2,1)} %reshape.174), calls=%async_computation.3 | async-start | bytes 1048576 | tf_op jit(solution)/shard_map/all_to_all | solution.py:125
  261.6 19.6 %all-to-all-start.2 = ((bf16[32,2,4096]{2,1,0:T(2,128)(2,1)}), bf16[32,2,4096]{2,1,0:T(2,128)(2,1)}, u32[]{:S(2)}, u32[]{:S(2)}) async-start(bf16[32,2,4096]{2,1,0:T(2,128)(2,1)} %reshape.172), calls=%async_computation.2 | async-start | bytes 1048576 | tf_op jit(solution)/shard_map/all_to_all | solution.py:122
  308.8 0.8 copy-start.10
  308.8 3.6 %copy-start.1 = (bf16[1024,128]{1,0:T(8,128)(2,1)S(1)}, bf16[1024,128]{1,0:T(8,128)(2,1)}, u32[]{:S(2)}) copy-start(bf16[1024,128]{1,0:T(8,128)(2,1)} %param.11) | copy-start | bytes 786436
Sparse Core Ops, SparseCore 0:
  12.2 28.1 all-gather.3
  96.9 46.1 all-gather.5
  145.0 67.7 all-gather.7
where the time goes:
time: 321 us; the launch traced here: 319 us
  waiting for transfers between devices  137 us (43%)
  local copies, waits for them, and re-layouts  75.2 us (23%)
  blocking collectives  52 us (16%)
  matrix products  23 us (7%)
  between operations  13.5 us (4%)
  starting transfers between devices  11.6 us (4%)
  other arithmetic  6.54 us (2%)
    all_gather x1, waiting for transfers between devices, local(): lax.all_gather(left_factor, 'col', axis=1, tiled=True)  64.6 us
    all_gather x1, waiting for transfers between devices, local(): col_panel = lax.all_gather(right_factor, 'row', axis=0, tiled=True)  45.5 us
    all_to_all x1, blocking collectives, local(): lax.all_to_all(all_tokens, 'row', split_axis=1, concat_axis=0, tiled=True)  22.2 us
    reshape x1, local copies, waits for them, and re-layouts, local(): outer_mean = (outer_sum / seq_total).astype(jnp.bfloat16).reshape(row_tok...  19.5 us
    all_to_all x1, blocking collectives, local(): lax.all_to_all(split_tiles(mixed_full, row_count, col_count, row_tokens,...  18.3 us
    transpose x1, local copies, waits for them, and re-layouts, local(): outer_mean.transpose(0, 2, 1, 3)  16 us
    all_to_all x1, waiting for transfers between devices, local(): lax.all_to_all(channel_major(right_factor), ('row', 'col'), split_axis=0,...  13.1 us
    all_to_all x1, waiting for transfers between devices, local(): lax.all_to_all(channel_major(left_factor), ('row', 'col'), split_axis=0,...  13.1 us
  transfers between devices with their start and end apart: 6, of which 4 were waited for; matrix products, arithmetic and copies ran while one was open for 3% of the time, Pallas kernels for 0%

commit v1 on v0

v1 whole, which is shorter than its diff:
```python
import functools

import jax
import jax.numpy as jnp
from jax import lax
from jax.experimental import pallas as pl
from jax.experimental.pallas import tpu as pltpu
from jax.sharding import PartitionSpec as P

EPS = 1e-05
LANES = 128
F32 = jnp.float32
BF16 = jnp.bfloat16


def contract(a, b, dim_a, dim_b):
    return lax.dot_general(a, b, (((dim_a,), (dim_b,)), ((), ())), preferred_element_type=F32)


def iota(shape, dim):
    return lax.broadcasted_iota(jnp.int32, shape, dim)


def call(kernel, out_shape, scratch, *args):
    return pl.pallas_call(
        kernel,
        out_shape=out_shape,
        in_specs=[pl.BlockSpec(memory_space=pltpu.VMEM)] * len(args),
        out_specs=jax.tree.map(lambda _: pl.BlockSpec(memory_space=pltpu.VMEM), out_shape),
        scratch_shapes=scratch,
    )(*args)


def factor_kernel(x_ref, w_ref, row_ref, col_ref):
    seq, width = x_ref.shape
    feats, both = w_ref.shape
    hid = both // 2
    per = LANES // hid
    span = per * feats
    groups = width // span
    blocks, _, row_width = row_ref.shape
    row_groups = row_width // LANES
    same = iota((span, span), 0) // feats == iota((span, span), 1) // feats
    spread = jnp.where(same, 1.0 / feats, 0.0).astype(BF16)
    x = jnp.concatenate([x_ref[:, g * span : (g + 1) * span] for g in range(groups)], axis=0)
    cen = x.astype(F32) - jnp.dot(x, spread, preferred_element_type=F32)
    sq = cen * cen
    high = sq.astype(BF16)
    low = (sq - high.astype(F32)).astype(BF16)
    var = jnp.dot(high, spread, preferred_element_type=F32) + jnp.dot(
        low, spread, preferred_element_type=F32
    )
    normed = (cen * lax.rsqrt(var + EPS)).astype(BF16)
    pick_rows = (iota((span, feats), 0) % feats == iota((span, feats), 1)).astype(BF16)
    col_id = iota((both, 2 * LANES), 1)
    pick_cols = (col_id // LANES * hid + col_id % hid == iota((both, 2 * LANES), 0)).astype(BF16)
    tall = jnp.dot(pick_rows, w_ref[...], preferred_element_type=F32).astype(BF16)
    wide = jnp.dot(tall, pick_cols, preferred_element_type=F32)
    mine = iota((span, 2 * LANES), 0) // feats == iota((span, 2 * LANES), 1) % LANES // hid
    weights = jnp.where(mine, wide, 0.0).astype(BF16)
    out = jnp.dot(normed, weights, preferred_element_type=F32).astype(BF16)
    for g in range(groups):
        piece = out[g * seq : (g + 1) * seq, :]
        at = g % row_groups * LANES
        row_ref[g // row_groups, :, at : at + LANES] = piece[:, :LANES]
        col_ref[:, g * LANES : (g + 1) * LANES] = piece[:, LANES:]


def widen_kernel(w_ref, out_ref, wide_ref, *, hid):
    per = LANES // hid
    channels = w_ref.shape[1]
    wide_ref[...] = w_ref[...].astype(F32)
    out_ref[...] = jnp.zeros_like(out_ref)
    for q in range(hid):
        part = wide_ref[pl.ds(q, hid, stride=hid), :].astype(BF16)
        for t in range(per):
            at = q * LANES + t * hid
            out_ref[at : at + hid, t * channels : (t + 1) * channels] = part


def normalize_rows(x):
    average = jnp.mean(x, axis=0, keepdims=True)
    cen = x - average
    return cen * lax.rsqrt(jnp.mean(cen * cen, axis=0, keepdims=True) + EPS)


def project(pair_ref, w_ref, lr_ref, gate_ref, left_ref, right_ref):
    channels, positions = pair_ref.shape
    groups = positions // LANES
    hid = (w_ref.shape[1] - channels) // 4
    count = lr_ref.shape[0]
    half = lr_ref.shape[1] // 2
    step = 4 * LANES
    for at in range(0, positions, step):
        normed = normalize_rows(pair_ref[:, at : at + step]).astype(BF16)

        def cols(begin, end):
            return contract(w_ref[:, begin:end], normed, 0, 0)

        left = jax.nn.sigmoid(cols(0, hid)) * cols(hid, 2 * hid)
        right = jax.nn.sigmoid(cols(2 * hid, 3 * hid)) * cols(3 * hid, 4 * hid)
        gate_ref[:, at : at + step] = jax.nn.sigmoid(cols(4 * hid, 4 * hid + channels))
        for g in range(at // LANES, (at + step) // LANES):
            lane = g * LANES - at
            left_ref[pl.ds(g, hid, stride=groups), :] = left[:, lane : lane + LANES]
            right_ref[pl.ds(g, hid, stride=groups), :] = right[:, lane : lane + LANES]
    lr_ref[:, :half, :] = left_ref[...].astype(BF16).reshape(count, half, LANES)
    lr_ref[:, half:, :] = right_ref[...].astype(BF16).reshape(count, half, LANES)


def opm_kernel(
    row_ref,
    col_ref,
    wide_ref,
    state_ref,
    w_ref,
    pair_ref,
    lr_ref,
    gate_ref,
    row_scr,
    outer_scr,
    lhs_scr,
    left_scr,
    right_scr,
    *,
    hid,
):
    blocks, seq, row_width = row_ref.shape
    row_tokens, col_tokens, channels = state_ref.shape
    total = blocks * seq
    per = LANES // hid
    mine = lax.axis_index("row")
    for m in range(blocks):
        row_scr[m * seq : (m + 1) * seq, :] = row_ref[mine ^ m]
    pack = LANES // col_tokens
    groups = row_tokens // per
    pairs = groups // pack
    tall = col_tokens * hid
    outer = contract(col_ref[...].reshape(total, tall), row_scr[...], 0, 0)
    for g in range(groups):
        outer_scr[g * tall : (g + 1) * tall, :] = outer[:, g * LANES : (g + 1) * LANES]
    for q in range(hid):
        for g in range(groups):
            part = outer_scr[pl.ds(g * tall + q, col_tokens, stride=hid), :] * (1.0 / total)
            at = (g % pairs * pack + g // pairs) * col_tokens
            lhs_scr[at : at + col_tokens, q * LANES : (q + 1) * LANES] = part.astype(BF16)
    term = jnp.dot(lhs_scr[...], wide_ref[...], preferred_element_type=F32)
    half = row_tokens // pack
    for g in range(pairs):
        for t in range(per):
            token = g * per + t
            block = term[g * LANES : (g + 1) * LANES, t * channels : (t + 1) * channels]
            state = jnp.concatenate([state_ref[token + h * half] for h in range(pack)], axis=0)
            pair_ref[:, token * LANES : (token + 1) * LANES] = (block + state).T
    project(pair_ref, w_ref, lr_ref, gate_ref, left_scr, right_scr)


def mix_kernel(lr_ref, out_ref, left_scr, right_scr, *, rows, cols, row_tokens, col_tokens, outgoing):
    pack = LANES // col_tokens
    half = row_tokens // pack
    share = out_ref.shape[1] // half
    for e in range(share):
        for part, scr in enumerate((left_scr, right_scr)):
            at = (part * share + e) * half
            for r in range(rows):
                for m in range(cols // pack):
                    tiles = [
                        lr_ref[r * cols + m * pack + b, at : at + half, :] for b in range(pack)
                    ]
                    for h in range(pack):
                        joined = jnp.concatenate(
                            [tile[:, h * col_tokens : (h + 1) * col_tokens] for tile in tiles], axis=1
                        )
                        first = r * row_tokens + h * half
                        scr[first : first + half, m * LANES : (m + 1) * LANES] = joined
        dim = 1 if outgoing else 0
        mixed = contract(left_scr[...], right_scr[...], dim, dim).astype(BF16)
        for r in range(rows):
            for m in range(cols // pack):
                tiles = [
                    mixed[
                        r * row_tokens + h * half : r * row_tokens + (h + 1) * half,
                        m * LANES : (m + 1) * LANES,
                    ]
                    for h in range(pack)
                ]
                for b in range(pack):
                    joined = jnp.concatenate(
                        [tile[:, b * col_tokens : (b + 1) * col_tokens] for tile in tiles], axis=1
                    )
                    out_ref[r * cols + m * pack + b, e * half : (e + 1) * half, :] = joined


def normalize_mix(mix_ref, scr, hid, groups):
    mixed = mix_ref[...].reshape(hid, groups, LANES).astype(F32)
    average = jnp.mean(mixed, axis=0, keepdims=True)
    cen = mixed - average
    spread = jnp.mean(cen * cen, axis=0, keepdims=True)
    scr[...] = (cen * lax.rsqrt(spread + EPS)).reshape(hid * groups, LANES)


def update_group(scr, final_ref, g, groups):
    hid = final_ref.shape[0]
    normed = scr[pl.ds(g, hid, stride=groups), :].astype(BF16)
    return contract(final_ref[...], normed, 0, 0)


def finish_kernel(
    mix_ref, pair_ref, gate_ref, final_ref, w_ref, mid_ref, lr_ref, gate_out_ref, scr, left_scr, right_scr
):
    hid = final_ref.shape[0]
    groups = pair_ref.shape[1] // LANES
    normalize_mix(mix_ref, scr, hid, groups)
    for g in range(groups):
        at = slice(g * LANES, (g + 1) * LANES)
        mid_ref[:, at] = pair_ref[:, at] + gate_ref[:, at] * update_group(scr, final_ref, g, groups)
    project(mid_ref, w_ref, lr_ref, gate_out_ref, left_scr, right_scr)


def last_kernel(mix_ref, pair_ref, gate_ref, final_ref, out_ref, scr):
    hid = final_ref.shape[0]
    row_tokens, col_tokens, _ = out_ref.shape
    groups = pair_ref.shape[1] // LANES
    pack = LANES // col_tokens
    normalize_mix(mix_ref, scr, hid, groups)
    for g in range(groups):
        at = slice(g * LANES, (g + 1) * LANES)
        done = pair_ref[:, at] + gate_ref[:, at] * update_group(scr, final_ref, g, groups)
        done = done.T
        for h in range(pack):
            out_ref[g + h * groups] = done[h * col_tokens : (h + 1) * col_tokens, :]


def gather_blocks(block, rows):
    far = [block] + [
        lax.ppermute(block, "row", [(i, i ^ m) for i in range(rows)]) for m in range(2, rows, 2)
    ]
    far = jnp.stack(far)
    near = lax.ppermute(far, "row", [(i, i ^ 1) for i in range(rows)])
    return jnp.stack([far, near], axis=1).reshape((rows,) + block.shape)


def local(
    alignment,
    pair_state,
    alignment_factor_weight,
    outer_proj,
    outgoing_proj,
    outgoing_final,
    incoming_proj,
    incoming_final,
):
    seq = alignment.shape[0]
    row_tokens, col_tokens, channels = pair_state.shape
    hid_outer = alignment_factor_weight.shape[1] // 2
    hid = outgoing_final.shape[0]
    rows, cols = lax.axis_size("row"), lax.axis_size("col")
    count = rows * cols
    total = rows * seq
    per = LANES // hid_outer
    positions = row_tokens * col_tokens
    groups = positions // LANES
    both = ("row", "col")
    shape = jax.ShapeDtypeStruct

    row_source, col_source = call(
        factor_kernel,
        (
            shape((col_tokens // row_tokens, seq, row_tokens * hid_outer), BF16),
            shape((seq, col_tokens * hid_outer), BF16),
        ),
        [],
        alignment,
        alignment_factor_weight,
    )
    wide = call(
        functools.partial(widen_kernel, hid=hid_outer),
        shape((hid_outer * LANES, per * channels), BF16),
        [pltpu.VMEM(outer_proj.shape, F32)],
        outer_proj,
    )
    col_all = gather_blocks(col_source, rows)
    row_all = lax.all_gather(row_source, "col", axis=0, tiled=True)
    row_all = lax.all_to_all(row_all, "row", split_axis=0, concat_axis=0, tiled=True)

    state = shape((channels, positions), F32)
    wire = shape((count, 2 * hid // count * groups, LANES), BF16)
    turned = pltpu.VMEM((hid * groups, LANES), F32)
    pair, factors, gate = call(
        functools.partial(opm_kernel, hid=hid_outer),
        (state, wire, state),
        [
            pltpu.VMEM((total, row_tokens * hid_outer), BF16),
            pltpu.VMEM((positions * hid_outer * hid_outer // LANES, LANES), F32),
            pltpu.VMEM((positions // per, hid_outer * LANES), BF16),
            turned,
            turned,
        ],
        row_all,
        col_all,
        wide,
        pair_state,
        outgoing_proj,
    )

    def mix(factors, outgoing):
        factors = lax.all_to_all(factors, both, split_axis=0, concat_axis=0, tiled=True)
        whole = (rows * row_tokens, cols * col_tokens)
        mixed = call(
            functools.partial(
                mix_kernel,
                rows=rows,
                cols=cols,
                row_tokens=row_tokens,
                col_tokens=col_tokens,
                outgoing=outgoing,
            ),
            shape((count, hid // count * groups, LANES), BF16),
            [pltpu.VMEM(whole, BF16)] * 2,
            factors,
        )
        return lax.all_to_all(mixed, both, split_axis=0, concat_axis=0, tiled=True)

    pair, factors, gate = call(
        finish_kernel,
        (state, wire, state),
        [turned, turned, turned],
        mix(factors, True),
        pair,
        gate,
        outgoing_final,
        incoming_proj,
    )
    return call(
        last_kernel,
        shape(pair_state.shape, F32),
        [turned],
        mix(factors, False),
        pair,
        gate,
        incoming_final,
    )


def solution(mesh):
    return jax.shard_map(
        local,
        mesh=mesh,
        in_specs=(P("row", "col"), P("row", "col", None), P(), P(), P(), P(), P(), P()),
        out_specs=P("row", "col", None),
        check_vma=False,
    )
```

time: 321 us -> 171 us (0.53)
  waiting for transfers between devices: 137 us -> 9 us
  local copies, waits for them, and re-layouts: 75.2 us -> 1.84 us
  blocking collectives: 52 us -> 111 us
  Pallas kernels: 0 us -> 35.9 us
  matrix products: 23 us -> 0 us
  between operations: 13.5 us -> 0.04 us
  other arithmetic: 6.54 us -> 1.09 us
    all_gather x3 -> x0, waiting for transfers between devices: 110 us -> none  [the longest x1 64.6 us: local(): lax.all_gather(left_factor, 'col', axis=1, tiled=True)]
    all_to_all x2 -> x4, blocking collectives: 40.5 us -> 99.1 us  [the longest x2 59.8 us: mix(): lax.all_to_all(factors, both, split_axis=0, concat_axis=0, tiled=True)]
    pallas_call x0 -> x7, Pallas kernels: none -> 35.9 us  [call(): pl.pallas_call(kernel, out_shape=out_shape, in_specs=[pl.BlockSpec(memory...]
    reshape x10 -> x0, local copies, waits for them, and re-layouts: 27.1 us -> none  [the longest x1 19.5 us: local(): outer_mean = (outer_sum / seq_total).astype(jnp.bfloat16).reshape(row_tok...]
    dot_general x9 -> x0, matrix products: 23 us -> none  [the longest x1 5.97 us: local(): jnp.dot(outer_mean, outer_proj, preferred_element_type=jnp.float32)]
    transpose x3 -> x0, local copies, waits for them, and re-layouts: 19.3 us -> none  [the longest x1 16 us: local(): outer_mean.transpose(0, 2, 1, 3)]
    all_to_all x3 -> x1, waiting for transfers between devices: 26.2 us -> 8.99 us  [local(): lax.all_to_all(row_all, 'row', split_axis=0, concat_axis=0, tiled=True)]
    all_to_all x3 -> x0, local copies, waits for them, and re-layouts: 12.5 us -> none  [the longest x2 12.4 us: local(): lax.all_to_all(col_panel, 'col', split_axis=0, concat_axis=1, tiled=True)]
  transfers between devices with their start and end apart: 6 -> 5, of which waited for: 4 -> 1; matrix products, arithmetic and copies ran while one was open for 3% -> 1% of each run, Pallas kernels for 0% -> 2%
where the time goes in v1:
time: 171 us; the launch traced here: 170 us
  blocking collectives  111 us (65%)
  Pallas kernels  35.9 us (21%)
  starting transfers between devices  11.1 us (6%)
  waiting for transfers between devices  9 us (5%)
  local copies, waits for them, and re-layouts  1.84 us (1%)
    all_to_all x2, blocking collectives, mix(): lax.all_to_all(factors, both, split_axis=0, concat_axis=0, tiled=True)  59.8 us
    all_to_all x2, blocking collectives, mix(): return lax.all_to_all(mixed, both, split_axis=0, concat_axis=0, tiled=True)  39.4 us
    pallas_call x7, Pallas kernels, call(): pl.pallas_call(kernel, out_shape=out_shape, in_specs=[pl.BlockSpec(memory...  35.9 us
    all_gather x1, blocking collectives, local(): row_all = lax.all_gather(row_source, 'col', axis=0, tiled=True)  11.8 us
    all_to_all x1, waiting for transfers between devices, local(): lax.all_to_all(row_all, 'row', split_axis=0, concat_axis=0, tiled=True)  8.99 us
    ppermute x3, starting transfers between devices, gather_blocks(): lax.ppermute(block, 'row', [(i, i ^ m) for i in range(rows)])  5.64 us
    all_to_all x1, starting transfers between devices, local(): lax.all_to_all(row_all, 'row', split_axis=0, concat_axis=0, tiled=True)  4.88 us
  transfers between devices with their start and end apart: 5, of which 1 were waited for; matrix products, arithmetic and copies ran while one was open for 1% of the time, Pallas kernels for 2%

profile of v1, /device:TPU:0, one launch (start us, length us, event | category | flops | bytes accessed | tf_op | source)
XLA Modules:
  0.0 170.0 jit_solution(8279647173120426642)
XLA Ops:
  0.0 2.3 %shard_map.82 = (bf16[2,32,1024]{2,1,0:T(8,128)(2,1)}, bf16[32,2048]{1,0:T(8,128)(2,1)}) custom-call(bf16[32,4096]{1,0:T(8,128)(2,1)} %x_ref.1, bf16[64,64]{1,0:T(8,128)(2,1)} %w_ref.4), custom_call_target="tpu_custom_call" | custom-call | tf_op jit(solution)/shard_map/pallas_call | solution.py:25
  2.3 5.1 %collective-permute-start.2 = (bf16[32,2048]{1,0:T(8,128)(2,1)}, bf16[32,2048]{1,0:T(8,128)(2,1)S(1)}, u32[]{:S(2)}, u32[]{:S(2)}) collective-permute-start(bf16[32,2048]{1,0:T(8,128)(2,1)} %get-tuple-element.14), channel_id=1, source_target_pairs={{0,24},{4,28},{8,16},{12,20},{16,8},{20,12},{24,0},{28,4},{1,25},{... | collective-permute-start | bytes 393224 | tf_op jit(solution)/shard_map/ppermute | solution.py:236
  7.4 0.0 collective-permute-start.1
  7.4 0.6 collective-permute-start
  8.0 11.8 %all_gather.3 = bf16[8,32,1024]{2,1,0:T(8,128)(2,1)} all-gather(bf16[2,32,1024]{2,1,0:T(8,128)(2,1)} %get-tuple-element.13), channel_id=1, replica_groups=mesh['row'=8,'col'=4] {'col'}, dimensions={0}, use_global_device_ids=true | all-gather | bytes 655360 | tf_op jit(solution)/shard_map/all_gather | solution.py:283
  19.8 4.9 %all-to-all-start = ((bf16[8,32,1024]{2,1,0:T(8,128)(2,1)}), bf16[8,32,1024]{2,1,0:T(8,128)(2,1)S(1)}, u32[]{:S(2)}, u32[]{:S(2)}) async-start(bf16[8,32,1024]{2,1,0:T(8,128)(2,1)} %all_gather.3), calls=%async_computation | async-start | bytes 1048576 | tf_op jit(solution)/shard_map/all_to_all | solution.py:284
  24.7 0.0 collective-permute-done.2
  24.7 0.0 collective-permute-done.1
  24.7 0.0 collective-permute-done
  24.7 1.0 fusion
  25.7 0.6 collective-permute-start.3
  26.3 3.6 %shard_map.83.wide_ref = bf16[4096,512]{1,0:T(8,128)(2,1)} custom-call(bf16[1024,128]{1,0:T(8,128)(2,1)} %w_ref.5), custom_call_target="tpu_custom_call" | custom-call | tf_op jit(solution)/shard_map/pallas_call | solution.py:25
  29.9 0.0 collective-permute-done.3
  29.9 0.1 pad_maximum_fusion
  30.0 1.0 copy.10
  31.0 9.0 %all-to-all-done.row_ref = bf16[8,32,1024]{2,1,0:T(8,128)(2,1)S(1)} async-done(((bf16[8,32,1024]{2,1,0:T(8,128)(2,1)}), bf16[8,32,1024]{2,1,0:T(8,128)(2,1)S(1)}, u32[]{:S(2)}, u32[]{:S(2)}) %all-to-all-start) | async-done | bytes 524320 | tf_op jit(solution)/shard_map/all_to_all | solution.py:284
  40.0 0.0 copy-start
  40.0 0.8 copy-done
  40.8 15.1 %shard_map.84 = (f32[128,2048]{1,0:T(8,128)}, bf16[32,128,128]{2,1,0:T(8,128)(2,1)}, f32[128,2048]{1,0:T(8,128)}) custom-call(bf16[8,32,1024]{2,1,0:T(8,128)(2,1)} %copy-done, bf16[8,32,2048]{2,1,0:T(8,128)(2,1)} %bitcast.8, bf16[4096,512]{1,0:T(8,128)(2,1)} %shard_map.83.wide_ref, f32[32,64,128]{2,1,0:T(8,128)} %state_ref.1, bf16[128,640]{1,0:T(8,128)(2,1)} %w_ref.6), custom_call_target="tpu_custom_call" | custom-call | tf_op jit(solution)/shard_map/pallas_call | solution.py:25
  56.0 29.9 %all_to_all.25.lr_ref = bf16[32,128,128]{2,1,0:T(8,128)(2,1)} all-to-all(bf16[32,128,128]{2,1,0:T(8,128)(2,1)} %get-tuple-element.15), channel_id=1, replica_groups=mesh['row'=8,'col'=4] {'row','col'}, dimensions={0} | all-to-all | bytes 2097152 | tf_op jit(solution)/shard_map/all_to_all | solution.py:307
  85.8 2.7 %shard_map.85 = bf16[32,64,128]{2,1,0:T(8,128)(2,1)} custom-call(bf16[32,128,128]{2,1,0:T(8,128)(2,1)} %all_to_all.25.lr_ref), custom_call_target="tpu_custom_call" | custom-call | tf_op jit(solution)/shard_map/pallas_call | solution.py:25
  88.5 19.8 %all_to_all.26.mix_ref = bf16[32,64,128]{2,1,0:T(8,128)(2,1)} all-to-all(bf16[32,64,128]{2,1,0:T(8,128)(2,1)} %shard_map.85), channel_id=1, replica_groups=mesh['row'=8,'col'=4] {'row','col'}, dimensions={0} | all-to-all | bytes 1048576 | tf_op jit(solution)/shard_map/all_to_all | solution.py:322
  108.3 5.2 %shard_map.86 = (f32[128,2048]{1,0:T(8,128)}, bf16[32,128,128]{2,1,0:T(8,128)(2,1)}, f32[128,2048]{1,0:T(8,128)}) custom-call(bf16[32,64,128]{2,1,0:T(8,128)(2,1)} %all_to_all.26.mix_ref, f32[128,2048]{1,0:T(8,128)} %get-tuple-element.16.pair_ref, f32[128,2048]{1,0:T(8,128)} %get-tuple-element.17.gate_ref, bf16[128,128]{1,0:T(8,128)(2,1)} %final_ref.2, ...), custom_call_target="tpu_custom_call" | custom-call | tf_op jit(solution)/shard_map/pallas_call | solution.py:25
  113.5 29.9 %all_to_all.27.lr_ref = bf16[32,128,128]{2,1,0:T(8,128)(2,1)} all-to-all(bf16[32,128,128]{2,1,0:T(8,128)(2,1)} %get-tuple-element.18), channel_id=1, replica_groups=mesh['row'=8,'col'=4] {'row','col'}, dimensions={0} | all-to-all | bytes 2097152 | tf_op jit(solution)/shard_map/all_to_all | solution.py:307
  143.4 3.2 %shard_map.87 = bf16[32,64,128]{2,1,0:T(8,128)(2,1)} custom-call(bf16[32,128,128]{2,1,0:T(8,128)(2,1)} %all_to_all.27.lr_ref), custom_call_target="tpu_custom_call" | custom-call | tf_op jit(solution)/shard_map/pallas_call | solution.py:25
  146.6 19.6 %all_to_all.28.mix_ref = bf16[32,64,128]{2,1,0:T(8,128)(2,1)} all-to-all(bf16[32,64,128]{2,1,0:T(8,128)(2,1)} %shard_map.87), channel_id=1, replica_groups=mesh['row'=8,'col'=4] {'row','col'}, dimensions={0} | all-to-all | bytes 1048576 | tf_op jit(solution)/shard_map/all_to_all | solution.py:322
  166.2 3.8 %shard_map.88 = f32[32,64,128]{2,1,0:T(8,128)} custom-call(bf16[32,64,128]{2,1,0:T(8,128)(2,1)} %all_to_all.28.mix_ref, f32[128,2048]{1,0:T(8,128)} %get-tuple-element.19.pair_ref, f32[128,2048]{1,0:T(8,128)} %get-tuple-element.20.gate_ref, bf16[128,128]{1,0:T(8,128)(2,1)} %final_ref.3), custom_call_target="tpu_custom_call" | custom-call | tf_op jit(solution)/shard_map/pallas_call | solution.py:25
Async XLA Ops:
  2.3 22.4 %collective-permute-start.2 = (bf16[32,2048]{1,0:T(8,128)(2,1)}, bf16[32,2048]{1,0:T(8,128)(2,1)S(1)}, u32[]{:S(2)}, u32[]{:S(2)}) collective-permute-start(bf16[32,2048]{1,0:T(8,128)(2,1)} %get-tuple-element.14), channel_id=1, source_target_pairs={{0,24},{4,28},{8,16},{12,20},{16,8},{20,12},{24,0},{28,4},{1,25},{... | collective-permute-start | bytes 393224 | tf_op jit(solution)/shard_map/ppermute | solution.py:236
  7.4 17.3 %collective-permute-start.1 = (bf16[32,2048]{1,0:T(8,128)(2,1)}, bf16[32,2048]{1,0:T(8,128)(2,1)S(1)}, u32[]{:S(2)}, u32[]{:S(2)}) collective-permute-start(bf16[32,2048]{1,0:T(8,128)(2,1)} %get-tuple-element.14), channel_id=1, source_target_pairs={{0,16},{4,20},{8,24},{12,28},{16,0},{20,4},{24,8},{28,12},{1,17},{... | collective-permute-start | bytes 393224 | tf_op jit(solution)/shard_map/ppermute | solution.py:236
  7.4 17.3 %collective-permute-start = (bf16[32,2048]{1,0:T(8,128)(2,1)}, bf16[32,2048]{1,0:T(8,128)(2,1)S(1)}, u32[]{:S(2)}, u32[]{:S(2)}) collective-permute-start(bf16[32,2048]{1,0:T(8,128)(2,1)} %get-tuple-element.14), channel_id=1, source_target_pairs={{0,8},{4,12},{8,0},{12,4},{16,24},{20,28},{24,16},{28,20},{1,9},{5... | collective-permute-start | bytes 393224 | tf_op jit(solution)/shard_map/ppermute | solution.py:236
  19.8 20.2 %all-to-all-start = ((bf16[8,32,1024]{2,1,0:T(8,128)(2,1)}), bf16[8,32,1024]{2,1,0:T(8,128)(2,1)S(1)}, u32[]{:S(2)}, u32[]{:S(2)}) async-start(bf16[8,32,1024]{2,1,0:T(8,128)(2,1)} %all_gather.3), calls=%async_computation | async-start | bytes 1048576 | tf_op jit(solution)/shard_map/all_to_all | solution.py:284
  25.7 4.2 %collective-permute-start.3 = (bf16[4,32,2048]{2,1,0:T(8,128)(2,1)S(1)}, bf16[4,32,2048]{2,1,0:T(8,128)(2,1)S(1)}, u32[]{:S(2)}, u32[]{:S(2)}) collective-permute-start(bf16[4,32,2048]{2,1,0:T(8,128)(2,1)S(1)} %get-tuple-element.22), channel_id=1, source_target_pairs={{0,4},{4,0},{8,12},{12,8},{16,20},{20,16},{24,28},{28,24},{1,5},{5... | collective-permute-start | bytes 1572872 | tf_op jit(solution)/shard_map/ppermute | solution.py:239
  40.0 0.8 copy-start
